TPU v7x, 256 devices: a whole 4x4x8 slice. The times are simulated.
256 devices in a mesh: src: 32 (over z, y), tgt: 8 (over x, core).
Axes of the slice: x: 4, y: 4, z: 8, core: 2. Of those that a mesh axis runs over, the one named last changes fastest.
Arguments:
- source: bfloat16 [32768, 300], P('src'), may hold values from -70 to 70
- target: bfloat16 [16384, 300], P('tgt'), may hold values from -11 to 11
- start_map: float32 [300, 300], replicated, may hold values from -1.5 to 1.5
Outputs:
- source_soft: bfloat16 [32768, 300], P(('src', 'tgt'))
- target_soft: bfloat16 [16384, 300], P('tgt')
- polar_map: float32 [300, 300], replicated
All inputs are finite; a program needn't handle non-finite values.
Results may differ from a plain program's by a relative error of at most 0.014.
The roundings to bfloat16 on the way count: a program that leaves them out, or rounds other values in their place, can miss the bound.
Values may be sent and summed in bfloat16 or wider, within the bound.
A program may use at most 64 MiB of HBM per device.

v0:
```python
import math
import jax
import jax.numpy as jnp
from jax import lax
from jax.sharding import PartitionSpec as P

ITERS = 2
NEWTON_STEPS = 8


def polar_steps(covariance):
    highest = lax.Precision.HIGHEST
    current = covariance / jnp.sqrt(jnp.sum(covariance * covariance) + 1e-06)
    for newton in range(NEWTON_STEPS):
        gram_matrix = jnp.dot(current.T, current, precision=highest)
        current = 1.5 * current - 0.5 * jnp.dot(current, gram_matrix, precision=highest)
    return current


def translation_sums(row_weights, col_weights, source, target, share_target, src_index):
    source_sum = lax.psum_scatter(
        jnp.dot(row_weights, target, preferred_element_type=jnp.float32),
        "tgt",
        scatter_dimension=0,
        tiled=True,
    )
    target_full = lax.psum(
        lax.dot_general(
            col_weights, source, (((0,), (0,)), ((), ())), preferred_element_type=jnp.float32
        ),
        "src",
    )
    target_sum = lax.dynamic_slice_in_dim(target_full, src_index * share_target, share_target, 0)
    return (source_sum, target_sum, target_full)


def body(source, target, start_map):
    highest = lax.Precision.HIGHEST
    score_scale = 2.0 / math.sqrt(source.shape[1])
    rows_source = source.shape[0]
    rows_target = target.shape[0]
    src_devices = lax.axis_size("src")
    tgt_devices = lax.axis_size("tgt")
    src_index = lax.axis_index("src")
    tgt_index = lax.axis_index("tgt")
    share_source = rows_source // tgt_devices
    share_target = rows_target // src_devices
    source_piece = lax.dynamic_slice_in_dim(
        source, tgt_index * share_source, share_source, 0
    ).astype(jnp.float32)
    target_piece = lax.dynamic_slice_in_dim(
        target, src_index * share_target, share_target, 0
    ).astype(jnp.float32)
    current = start_map
    source_sum = None
    target_sum = None
    target_full = None
    for iteration in range(ITERS):
        mapped = jnp.dot(
            source, current.astype(jnp.bfloat16), preferred_element_type=jnp.float32
        ).astype(jnp.bfloat16)
        scores = (
            lax.dot_general(
                mapped, target, (((1,), (1,)), ((), ())), preferred_element_type=jnp.float32
            )
            * score_scale
        )
        row_local = jnp.max(scores, axis=1)
        col_local = jnp.max(scores, axis=0)
        row_top = lax.pmax(row_local, "tgt")
        col_top = lax.pmax(col_local, "src")
        row_total = lax.psum(jnp.sum(jnp.exp(scores - row_top[:, None]), axis=1), "tgt")
        col_total = lax.psum(jnp.sum(jnp.exp(scores - col_top[None, :]), axis=0), "src")
        row_weights = (jnp.exp(scores - row_top[:, None]) / row_total[:, None]).astype(jnp.bfloat16)
        col_weights = (jnp.exp(scores - col_top[None, :]) / col_total[None, :]).astype(jnp.bfloat16)
        source_sum, target_sum, target_full = translation_sums(
            row_weights, col_weights, source, target, share_target, src_index
        )
        covariance = jnp.dot(source_piece.T, source_sum, precision=highest)
        covariance = covariance + jnp.dot(target_sum.T, target_piece, precision=highest)
        covariance = lax.psum(covariance, ("src", "tgt"))
        current = polar_steps(covariance)
    source_share = source_sum.astype(jnp.bfloat16)
    target_soft = target_full.astype(jnp.bfloat16)
    return (source_share, target_soft, current)


def solution(mesh):
    in_specs = (P("src", None), P("tgt", None), P())
    out_specs = (P(("src", "tgt"), None), P("tgt", None), P())
    return jax.shard_map(body, mesh=mesh, in_specs=in_specs, out_specs=out_specs, check_vma=False)
```

profile of v0, /device:TPU:2, one launch (start us, length us, event | category | flops | bytes accessed | tf_op | source)
XLA Modules:
  0.0 1263.8 jit_solution(214851185553863919)
XLA Ops:
  9.3 7.3 multiply_reduce_fusion.2
  16.6 78.9 %pmax.29 = f32[2048]{0:T(1024)S(1)} all-reduce(f32[2048]{0:T(1024)S(1)} %get-tuple-element.9), channel_id=1, replica_groups=mesh['src'=32,'tgt'=8] {'src'}, use_global_device_ids=true, to_apply=%region_6.0 | all-reduce | flops 2048 | bytes 16384 | tf_op jit(solution)/shard_map/pmax | solution.py:71
  95.5 10.0 pmax.28
  105.6 5.2 fusion.1
  110.8 12.4 psum.56
  123.2 7.0 fusion.6
  130.3 70.6 %psum.57 = f32[2048]{0:T(1024)S(1)} all-reduce(f32[2048]{0:T(1024)S(1)} %get-tuple-element.7), channel_id=1, replica_groups=mesh['src'=32,'tgt'=8] {'src'}, use_global_device_ids=true, to_apply=%region_8.0 | all-reduce | flops 2048 | bytes 16384 | tf_op jit(solution)/shard_map/psum | solution.py:73
  201.0 7.6 fusion.4
  210.0 153.4 %all-reduce.5.cloned.1.call-done = f32[2048,300]{1,0:T(8,128)} async-done(((f32[2048,300]{1,0:T(8,128)}), f32[2048,300]{1,0:T(8,128)}) %all-reduce.5.cloned.1.call-update) | async-done | bytes 2457616 | tf_op jit(solution)/shard_map/psum | solution.py:27
  365.8 248.9 %all-reduce.7.cloned.1.call-done = f32[300,300]{1,0:T(8,128)} async-done(((f32[300,300]{1,0:T(8,128)}), f32[300,300]{1,0:T(8,128)}) %all-reduce.7.cloned.1.call-update) | async-done | bytes 360016 | tf_op jit(solution)/shard_map/psum | solution.py:81
  617.1 2.4 fusion.29
  638.2 5.3 multiply_reduce_fusion
  643.5 72.1 %pmax.31 = f32[2048]{0:T(1024)S(1)} all-reduce(f32[2048]{0:T(1024)S(1)} %get-tuple-element.5), channel_id=1, replica_groups=mesh['src'=32,'tgt'=8] {'src'}, use_global_device_ids=true, to_apply=%region_18.0 | all-reduce | flops 2048 | bytes 16384 | tf_op jit(solution)/shard_map/pmax | solution.py:71
  715.6 10.0 pmax.30
  725.6 5.2 fusion.3
  730.9 12.6 %psum.60 = f32[1024]{0:T(1024)S(1)} all-reduce(f32[1024]{0:T(1024)S(1)} %get-tuple-element.4), channel_id=1, replica_groups=mesh['src'=32,'tgt'=8] {'tgt'}, use_global_device_ids=true, to_apply=%region_15.0 | all-reduce | flops 1024 | bytes 8192 | tf_op jit(solution)/shard_map/psum | solution.py:72
  743.5 6.4 fusion.7
  750.0 70.8 %psum.61 = f32[2048]{0:T(1024)S(1)} all-reduce(f32[2048]{0:T(1024)S(1)} %get-tuple-element.3), channel_id=1, replica_groups=mesh['src'=32,'tgt'=8] {'src'}, use_global_device_ids=true, to_apply=%region_20.0 | all-reduce | flops 2048 | bytes 16384 | tf_op jit(solution)/shard_map/psum | solution.py:73
  820.8 6.8 fusion.5
  829.2 151.9 %all-reduce.9.cloned.1.call-done = f32[2048,300]{0,1:T(8,128)} async-done(((f32[2048,300]{0,1:T(8,128)}), f32[2048,300]{0,1:T(8,128)}) %all-reduce.9.cloned.1.call-update) | async-done | bytes 2457616 | tf_op jit(solution)/shard_map/psum | solution.py:27
  984.8 2.9 convert_element_type.42
  987.7 244.7 %all-reduce.11.cloned.1.call-done = f32[300,300]{1,0:T(8,128)} async-done(((f32[300,300]{1,0:T(8,128)}), f32[300,300]{1,0:T(8,128)}) %all-reduce.11.cloned.1.call-update) | async-done | bytes 360016 | tf_op jit(solution)/shard_map/psum | solution.py:81
  1234.8 2.4 fusion.30
  1237.2 2.2 fusion.17
  (54 shorter events, 49.3 us)
Async XLA Ops:
  8.0 1.3 copy-start
  8.0 200.7 %reduce-scatter.3.cloned.1.call-start = ((), (), s32[]{:S(2)}) async-start(), calls=%async_computation.2 | async-start | bytes 1769472 | tf_op jit(solution)/shard_map/reduce_scatter | solution.py:21
  123.2 77.8 %copy-start.1 = (bf16[1024,300]{0,1:T(8,128)(2,1)S(1)}, bf16[1024,300]{0,1:T(8,128)(2,1)}, u32[]{:S(2)}) copy-start(bf16[1024,300]{0,1:T(8,128)(2,1)} %param.3) | copy-start | bytes 1843204
  130.3 233.1 %all-reduce.5.cloned.1.call-start = ((), (), s32[]{:S(2)}) async-start(), calls=%async_computation.3 | async-start | bytes 6291456 | tf_op jit(solution)/shard_map/psum | solution.py:27
  208.6 406.1 %all-reduce.7.cloned.1.call-start = ((), (), s32[]{:S(2)}) async-start(), calls=%async_computation.4 | async-start | bytes 933888 | tf_op jit(solution)/shard_map/psum | solution.py:81
  365.5 462.4 %reduce-scatter.5.cloned.1.call-start = ((), (), s32[]{:S(2)}) async-start(), calls=%async_computation.5 | async-start | bytes 1400832 | tf_op jit(solution)/shard_map/reduce_scatter | solution.py:21
  749.9 231.1 %all-reduce.9.cloned.1.call-start = ((), (), s32[]{:S(2)}) async-start(), calls=%async_computation.6 | async-start | bytes 4980736 | tf_op jit(solution)/shard_map/psum | solution.py:27
  827.7 404.7 %all-reduce.11.cloned.1.call-start = ((), (), s32[]{:S(2)}) async-start(), calls=%async_computation.7 | async-start | bytes 933888 | tf_op jit(solution)/shard_map/psum | solution.py:81
Sparse Core Ops, SparseCore 0:
  130.4 26.5 reduce-scatter.2
  365.6 248.9 all-reduce.6
  750.1 27.8 reduce-scatter.4
  983.3 249.0 all-reduce.10
Sparse Core Ops, SparseCore 1:
  208.7 154.6 all-reduce.4
  827.8 153.2 all-reduce.8
where the time goes:
time: 1270 us; the launch traced here: 1260 us
  waiting for transfers between devices  799 us (63%)
  blocking collectives  338 us (27%)
  matrix products  89.8 us (7%)
  other arithmetic  18.4 us (1%)
  between operations  17.2 us (1%)
    psum x2, waiting for transfers between devices, body(): covariance = lax.psum(covariance, ('src', 'tgt'))  494 us
    psum x2, waiting for transfers between devices, translation_sums(): lax.psum(lax.dot_general(col_weights, source, (((0,), (0,)), ((), ())), p...  305 us
    pmax x2, blocking collectives, body(): col_top = lax.pmax(col_local, 'src')  151 us
    psum x2, blocking collectives, body(): lax.psum(jnp.sum(jnp.exp(scores - col_top[None, :]), axis=0), 'src')  141 us
  transfers between devices with their start and end apart: 6, of which 4 were waited for; matrix products, arithmetic and copies ran while one was open for 2% of the time, Pallas kernels for 0%

commit v1 on v0

--- a/solution.py
+++ b/solution.py
@@ -78,7 +78,7 @@
         )
         covariance = jnp.dot(source_piece.T, source_sum, precision=highest)
         covariance = covariance + jnp.dot(target_sum.T, target_piece, precision=highest)
-        covariance = lax.psum(covariance, ("src", "tgt"))
+        covariance = lax.psum(lax.psum(covariance, axis_name="tgt"), axis_name="src")
         current = polar_steps(covariance)
     source_share = source_sum.astype(jnp.bfloat16)
     target_soft = target_full.astype(jnp.bfloat16)

time: 1270 us -> 1200 us (0.945)
  waiting for transfers between devices: 799 us -> 719 us
    psum x2 -> x4, waiting for transfers between devices: 494 us -> 413 us  [the longest x2 293 us: body(): lax.psum(lax.psum(covariance, axis_name='tgt'), axis_name='src')]
  transfers between devices with their start and end apart: 6 -> 8, of which waited for: 4 -> 6; matrix products, arithmetic and copies ran while one was open for 2% -> 2% of each run, Pallas kernels for 0% -> 0%
where the time goes in v1:
time: 1200 us
  waiting for transfers between devices  719 us (60%)
  blocking collectives  338 us (28%)
  matrix products  99.4 us (8%)
  other arithmetic  18.4 us (2%)
  between operations  17.7 us (1%)
    psum x2, waiting for transfers between devices, translation_sums(): lax.psum(lax.dot_general(col_weights, source, (((0,), (0,)), ((), ())), p...  306 us
    psum x2, waiting for transfers between devices, body(): lax.psum(lax.psum(covariance, axis_name='tgt'), axis_name='src')  293 us
    pmax x2, blocking collectives, body(): col_top = lax.pmax(col_local, 'src')  152 us
    psum x2, blocking collectives, body(): lax.psum(jnp.sum(jnp.exp(scores - col_top[None, :]), axis=0), 'src')  141 us
    psum x2, waiting for transfers between devices, body(): lax.psum(covariance, axis_name='tgt')  120 us
    dot_general x16, matrix products, polar_steps(): gram_matrix = jnp.dot(current.T, current, precision=highest)  32.4 us
    psum x2, blocking collectives, body(): lax.psum(jnp.sum(jnp.exp(scores - row_top[:, None]), axis=1), 'tgt')  24.8 us
  transfers between devices with their start and end apart: 8, of which 6 were waited for; matrix products, arithmetic and copies ran while one was open for 2% of the time, Pallas kernels for 0%

profile of v1, /device:TPU:2, one launch (start us, length us, event | category | flops | bytes accessed | tf_op | source)
XLA Modules:
  0.0 1195.1 jit_solution(2195208333994970090)
XLA Ops:
  9.3 7.3 multiply_reduce_fusion.2
  16.6 78.9 %pmax.29 = f32[2048]{0:T(1024)S(1)} all-reduce(f32[2048]{0:T(1024)S(1)} %get-tuple-element.9), channel_id=1, replica_groups=mesh['src'=32,'tgt'=8] {'src'}, use_global_device_ids=true, to_apply=%region_6.0 | all-reduce | flops 2048 | bytes 16384 | tf_op jit(solution)/shard_map/pmax | solution.py:71
  95.5 10.0 pmax.28
  105.6 5.2 fusion.1
  110.8 12.4 %psum.70 = f32[1024]{0:T(1024)S(1)} all-reduce(f32[1024]{0:T(1024)S(1)} %get-tuple-element.8), channel_id=1, replica_groups=mesh['src'=32,'tgt'=8] {'tgt'}, use_global_device_ids=true, to_apply=%region_3.0 | all-reduce | flops 1024 | bytes 8192 | tf_op jit(solution)/shard_map/psum | solution.py:72
  123.2 7.0 fusion.6
  130.3 70.6 %psum.71 = f32[2048]{0:T(1024)S(1)} all-reduce(f32[2048]{0:T(1024)S(1)} %get-tuple-element.7), channel_id=1, replica_groups=mesh['src'=32,'tgt'=8] {'src'}, use_global_device_ids=true, to_apply=%region_8.0 | all-reduce | flops 2048 | bytes 16384 | tf_op jit(solution)/shard_map/psum | solution.py:73
  201.0 7.6 fusion.4
  210.0 153.3 %all-reduce.7.cloned.1.call-done = f32[2048,300]{1,0:T(8,128)} async-done(((f32[2048,300]{1,0:T(8,128)}), f32[2048,300]{1,0:T(8,128)}) %all-reduce.7.cloned.1.call-update) | async-done | bytes 2457616 | tf_op jit(solution)/shard_map/psum | solution.py:27
  365.5 60.0 %all-reduce.9.cloned.1.call-done = f32[300,300]{1,0:T(8,128)} async-done(((f32[300,300]{1,0:T(8,128)}), f32[300,300]{1,0:T(8,128)}) %all-reduce.9.cloned.1.call-update) | async-done | bytes 360016 | tf_op jit(solution)/shard_map/psum | solution.py:81
  425.8 148.8 %all-reduce.11.cloned.1.call-done = f32[300,300]{1,0:T(8,128)} async-done(((f32[300,300]{1,0:T(8,128)}), f32[300,300]{1,0:T(8,128)}) %all-reduce.11.cloned.1.call-update) | async-done | bytes 360016 | tf_op jit(solution)/shard_map/psum | solution.py:81
  590.8 11.2 fusion.53
  607.7 5.3 multiply_reduce_fusion
  613.0 73.2 %pmax.31 = f32[2048]{0:T(1024)S(1)} all-reduce(f32[2048]{0:T(1024)S(1)} %get-tuple-element.5), channel_id=1, replica_groups=mesh['src'=32,'tgt'=8] {'src'}, use_global_device_ids=true, to_apply=%region_19.0 | all-reduce | flops 2048 | bytes 16384 | tf_op jit(solution)/shard_map/pmax | solution.py:71
  686.3 10.0 pmax.30
  696.3 5.2 fusion.3
  701.5 12.4 %psum.75 = f32[1024]{0:T(1024)S(1)} all-reduce(f32[1024]{0:T(1024)S(1)} %get-tuple-element.4), channel_id=1, replica_groups=mesh['src'=32,'tgt'=8] {'tgt'}, use_global_device_ids=true, to_apply=%region_16.0 | all-reduce | flops 1024 | bytes 8192 | tf_op jit(solution)/shard_map/psum | solution.py:72
  714.0 6.4 fusion.7
  720.5 70.6 %psum.76 = f32[2048]{0:T(1024)S(1)} all-reduce(f32[2048]{0:T(1024)S(1)} %get-tuple-element.3), channel_id=1, replica_groups=mesh['src'=32,'tgt'=8] {'src'}, use_global_device_ids=true, to_apply=%region_21.0 | all-reduce | flops 2048 | bytes 16384 | tf_op jit(solution)/shard_map/psum | solution.py:73
  791.1 6.8 fusion.5
  799.3 152.6 %all-reduce.13.cloned.1.call-done = f32[2048,300]{0,1:T(8,128)} async-done(((f32[2048,300]{0,1:T(8,128)}), f32[2048,300]{0,1:T(8,128)}) %all-reduce.13.cloned.1.call-update) | async-done | bytes 2457616 | tf_op jit(solution)/shard_map/psum | solution.py:27
  954.3 59.9 %all-reduce.15.cloned.1.call-done = f32[300,300]{1,0:T(8,128)} async-done(((f32[300,300]{1,0:T(8,128)}), f32[300,300]{1,0:T(8,128)}) %all-reduce.15.cloned.1.call-update) | async-done | bytes 360016 | tf_op jit(solution)/shard_map/psum | solution.py:81
  1015.7 2.9 convert_element_type.42
  1018.6 144.6 %all-reduce.17.cloned.1.call-done = f32[300,300]{1,0:T(8,128)} async-done(((f32[300,300]{1,0:T(8,128)}), f32[300,300]{1,0:T(8,128)}) %all-reduce.17.cloned.1.call-update) | async-done | bytes 360016 | tf_op jit(solution)/shard_map/psum | solution.py:81
  (60 shorter events, 55.0 us)
Async XLA Ops:
  8.0 1.3 copy-start
  8.0 200.7 %reduce-scatter.3.cloned.1.call-start = ((), (), s32[]{:S(2)}) async-start(), calls=%async_computation.2 | async-start | bytes 1769472 | tf_op jit(solution)/shard_map/reduce_scatter | solution.py:21
  123.2 77.8 %copy-start.1 = (bf16[1024,300]{0,1:T(8,128)(2,1)S(1)}, bf16[1024,300]{0,1:T(8,128)(2,1)}, u32[]{:S(2)}) copy-start(bf16[1024,300]{0,1:T(8,128)(2,1)} %param.3) | copy-start | bytes 1843204
  130.3 233.0 %all-reduce.7.cloned.1.call-start = ((), (), s32[]{:S(2)}) async-start(), calls=%async_computation.3 | async-start | bytes 6291456 | tf_op jit(solution)/shard_map/psum | solution.py:27
  208.6 216.9 %all-reduce.9.cloned.1.call-start = ((), (), s32[]{:S(2)}) async-start(), calls=%async_computation.4 | async-start | bytes 933888 | tf_op jit(solution)/shard_map/psum | solution.py:81
  365.5 209.1 %all-reduce.11.cloned.1.call-start = ((), (), s32[]{:S(2)}) async-start(), calls=%async_computation.5 | async-start | bytes 933888 | tf_op jit(solution)/shard_map/psum | solution.py:81
  425.5 372.5 %reduce-scatter.5.cloned.1.call-start = ((), (), s32[]{:S(2)}) async-start(), calls=%async_computation.6 | async-start | bytes 1400832 | tf_op jit(solution)/shard_map/reduce_scatter | solution.py:21
  720.4 231.5 %all-reduce.13.cloned.1.call-start = ((), (), s32[]{:S(2)}) async-start(), calls=%async_computation.7 | async-start | bytes 4980736 | tf_op jit(solution)/shard_map/psum | solution.py:27
  798.0 216.2 %all-reduce.15.cloned.1.call-start = ((), (), s32[]{:S(2)}) async-start(), calls=%async_computation.8 | async-start | bytes 933888 | tf_op jit(solution)/shard_map/psum | solution.py:81
  954.0 209.2 %all-reduce.17.cloned.1.call-start = ((), (), s32[]{:S(2)}) async-start(), calls=%async_computation.9 | async-start | bytes 933888 | tf_op jit(solution)/shard_map/psum | solution.py:81
Sparse Core Ops, SparseCore 0:
  130.4 26.5 reduce-scatter.2
  365.6 59.8 all-reduce.8
  720.5 28.2 reduce-scatter.4
  954.1 59.9 all-reduce.14
Sparse Core Ops, SparseCore 1:
  208.7 154.5 all-reduce.6
  425.6 148.9 all-reduce.10
  798.1 153.8 all-reduce.12
  1014.2 148.9 all-reduce.16
